TPU v7x, 256 devices: a whole 4x4x8 slice. The times are simulated.
256 devices in a mesh: row: 8 (over x, core), col: 4 (over z_lo), layer: 8 (over y, z_hi).
Axes of the slice: x: 4, y: 4, z: 8 (z_hi: 2, z_lo: 4; z = z_hi * 4 + z_lo), core: 2. Of those that a mesh axis runs over, the one named last changes fastest.
Arguments:
- a_tiles: bfloat16 [8192, 16384], P('row', ('layer', 'col')), may hold values from -6 to 6
- a_occupancy: int32 [64, 128], P('row', ('layer', 'col')), may hold values 0 or 1
- b_tiles: bfloat16 [16384, 8192], P(('layer', 'row'), 'col'), may hold values from -0.046875 to 0.046875
- b_occupancy: int32 [128, 64], P(('layer', 'row'), 'col'), may hold values 0 or 1
Outputs:
- product: float32 [8192, 8192], P(('row', 'layer'), 'col')
Inputs may be any that keep to these rules, and one draw needn't show every extreme that they name: `a_occupancy`: each entry is 0 (block absent) or 1 (block present). `b_occupancy`: each entry is 0 (block absent) or 1 (block present).
All inputs are finite; a program needn't handle non-finite values.
Results may differ from a plain program's by a relative error of at most 0.0003.
Values may be sent and summed in bfloat16 or wider, within the bound.
A program may use at most 64 MiB of HBM per device.

v0:
```python
import jax
import jax.numpy as jnp
from jax import lax
from jax.sharding import PartitionSpec as P

BLOCK = 128


def keep_blocks(values, occupancy):
    height, breadth = values.shape
    tiled = values.reshape(height // BLOCK, BLOCK, breadth // BLOCK, BLOCK)
    flags = occupancy.astype(values.dtype)
    return (tiled * flags[:, None, :, None]).reshape(height, breadth)


def per_device(a_tiles, a_occupancy, b_tiles, b_occupancy):
    a_kept = keep_blocks(a_tiles, a_occupancy)
    b_kept = keep_blocks(b_tiles, b_occupancy)
    b_slab = lax.all_gather(b_kept, "row", axis=0, tiled=True)
    partial_value = jnp.dot(
        lax.all_gather(a_kept, "col", axis=1, tiled=True),
        b_slab,
        preferred_element_type=jnp.float32,
    )
    return lax.psum_scatter(partial_value, "layer", scatter_dimension=0, tiled=True)


def solution(mesh):
    in_specs = (
        P("row", ("layer", "col")),
        P("row", ("layer", "col")),
        P(("layer", "row"), "col"),
        P(("layer", "row"), "col"),
    )
    out_specs = P(("row", "layer"), "col")
    return jax.shard_map(
        per_device, mesh=mesh, in_specs=in_specs, out_specs=out_specs, check_vma=False
    )
```

profile of v0, /device:TPU:1, one launch (start us, length us, event | category | flops | bytes accessed | tf_op | source)
XLA Modules:
  0.0 354.4 jit_solution(10024609637868433303)
XLA Ops:
  6.5 0.0 all-gather.3.cloned.1.call-start
  6.5 0.7 convert_element_type.6
  7.2 0.1 copy.5
  7.3 0.3 mul.22
  7.7 2.3 bitcast_multiply_fusion.1
  10.0 0.0 all-gather.3.cloned.1.call-update
  10.0 0.0 all-gather.5.cloned.1.call-start
  10.1 0.7 convert_element_type.7
  10.8 0.2 mul.25
  11.0 2.5 bitcast_multiply_fusion
  13.5 0.0 all-gather.5.cloned.1.call-update
  13.5 0.0 reduce-scatter.2.cloned.1.call-start
  13.6 84.1 %all-gather.3.cloned.1.call-done = bf16[1024,2048]{1,0:T(8,128)(2,1)} async-done(((bf16[1024,512]{1,0:T(8,128)(2,1)}), bf16[1024,2048]{1,0:T(8,128)(2,1)}) %all-gather.3.cloned.1.call-update) | async-done | bytes 4194320 | tf_op jit(solution)/shard_map/all_gather | solution.py:21
  97.7 54.8 %all-gather.5.cloned.1.call-done = bf16[2048,2048]{1,0:T(8,128)(2,1)} async-done(((bf16[256,2048]{1,0:T(8,128)(2,1)}), bf16[2048,2048]{1,0:T(8,128)(2,1)}) %all-gather.5.cloned.1.call-update) | async-done | bytes 8388624 | tf_op jit(solution)/shard_map/all_gather | solution.py:19
  152.5 14.5 %fusion = f32[1024,2048]{1,0:T(8,128)} fusion(bf16[1024,2048]{1,0:T(8,128)(2,1)} %all-gather.3.cloned.1.call-done, bf16[2048,2048]{1,0:T(8,128)(2,1)} %all-gather.5.cloned.1.call-done), kind=kOutput, calls=%fused_computation.2 | convolution fusion | flops 8589934592 | bytes 20971520 | tf_op jit(solution)/shard_map/dot_general | solution.py:20
  167.0 0.0 reduce-scatter.2.cloned.1.call-update
  167.0 180.8 %reduce-scatter.2.cloned.1.call-done = f32[128,2048]{1,0:T(8,128)} async-done(((f32[1024,2048]{1,0:T(8,128)}), f32[128,2048]{1,0:T(8,128)}) %reduce-scatter.2.cloned.1.call-update) | async-done | bytes 1048592 | tf_op jit(solution)/shard_map/reduce_scatter | solution.py:25
Async XLA Ops:
  6.5 91.2 %all-gather.3.cloned.1.call-start = ((), (), s32[]{:S(2)}) async-start(), calls=%async_computation.1 | async-start | bytes 5242880 | tf_op jit(solution)/shard_map/all_gather | solution.py:21
  10.0 142.5 %all-gather.5.cloned.1.call-start = ((), (), s32[]{:S(2)}) async-start(), calls=%async_computation.2 | async-start | bytes 9437184 | tf_op jit(solution)/shard_map/all_gather | solution.py:19
  13.5 334.3 %reduce-scatter.2.cloned.1.call-start = ((), (), s32[]{:S(2)}) async-start(), calls=%async_computation.3 | async-start | bytes 9437184 | tf_op jit(solution)/shard_map/reduce_scatter | solution.py:25
Sparse Core Ops, SparseCore 0:
  10.2 87.5 all-gather.2
  99.6 52.9 all-gather.4
  167.2 180.6 reduce-scatter.1
where the time goes:
time: 355 us; the launch traced here: 354 us
  waiting for transfers between devices  320 us (90%)
  matrix products  14.5 us (4%)
  between operations  13.1 us (4%)
  other arithmetic  6.23 us (2%)
    reduce_scatter x1, waiting for transfers between devices, per_device(): lax.psum_scatter(partial_value, 'layer', scatter_dimension=0, tiled=True)  181 us
    all_gather x1, waiting for transfers between devices, per_device(): lax.all_gather(a_kept, 'col', axis=1, tiled=True)  84.1 us
    all_gather x1, waiting for transfers between devices, per_device(): b_slab = lax.all_gather(b_kept, 'row', axis=0, tiled=True)  54.8 us
    dot_general x1, matrix products, per_device(): jnp.dot(lax.all_gather(a_kept, 'col', axis=1, tiled=True), b_slab, prefer...  14.5 us
  transfers between devices with their start and end apart: 3, of which 3 were waited for; matrix products, arithmetic and copies ran while one was open for 1% of the time, Pallas kernels for 0%

commit v1 on v0

v1 whole, which is shorter than its diff:
```python
import functools

import jax
import jax.numpy as jnp
from jax import lax
from jax.experimental import pallas as pl
from jax.experimental.pallas import tpu as pltpu
from jax.sharding import PartitionSpec as P

MESH = pl.DeviceIdType.MESH
BLOCK = 128
STEPS = 8
SUB = BLOCK // STEPS
LEVELS = 32767.0
TINY = 1e-30
TILE = 256
HALF = 1024
ORDER = (
    "E1L", "G0", "E2L", "G1", "E3L", "A0", "C0L", "A1", "C1L", "G2", "E1R", "G3",
    "A2", "C2L", "E2R", "G4", "G5", "A3", "C3L", "E3R", "C0R", "C1R", "C2R", "C3R",
    "G6", "G7", "A4", "C4L", "C4R", "A5", "C5L", "C5R", "D0", "D1", "A6", "C6L",
    "C6R", "D2", "D3", "Z0", "Z1", "Z2", "Z3", "A7", "C7L", "C7R", "D4", "Z4",
    "D5", "Z5", "D6", "Z6", "D7", "Z7", "F0", "F1", "F2", "F3", "F4", "F5",
    "F6", "F7",
)


def kernel(a_occ, b_occ, a_ref, b_ref, out_ref, a_slab, b_slab, part, sent, sent_scale, got, got_scale,
           held, z_sent, z_sent_scale, z_got, z_got_scale,
           a_plus, a_minus, a_recv, b_plus, b_minus, b_twin, b_recv, b_twin_recv,
           y_send, y_recv, y_send_s, y_recv_s, z_send, z_recv, z_send_s, z_recv_s):
    row, zl, layer = lax.axis_index("row"), lax.axis_index("col"), lax.axis_index("layer")
    x, core = row // 2, row % 2
    y, zh = layer // 2, layer % 2

    def x_peer(shift):
        return {"row": ((x + shift + 4) % 4) * 2 + core}

    twin = {"row": x * 2 + (1 - core)}

    def y_peer(shift):
        return {"layer": ((y + shift) % 4) * 2 + zh}

    z_peer = {"layer": y * 2 + (1 - zh)}

    barrier = pltpu.get_barrier_semaphore()
    greeted = [x_peer(1), x_peer(-1), twin, y_peer(1), y_peer(2), y_peer(3), z_peer]
    greeted += [{"col": (zl + 1) % 4}, {"col": (zl + 3) % 4}]
    for peer in greeted:
        pl.semaphore_signal(barrier, inc=1, device_id=peer, device_id_type=MESH)

    for i in range(8):
        for k in range(4):
            cols = pl.ds(k * BLOCK, BLOCK)
            flag = a_occ[k, i].astype(jnp.float32)
            kept = a_ref[i, :, :, cols].astype(jnp.float32) * flag
            a_slab[:, zl, i, :, cols] = kept.astype(jnp.bfloat16)
    for i in range(2):
        for j in range(16):
            cols = pl.ds(j * BLOCK, BLOCK)
            rows = pl.ds(i * BLOCK, BLOCK)
            flag = b_occ[i, j].astype(jnp.float32)
            kept = b_ref[rows, cols].astype(jnp.float32) * flag
            b_slab[row, i, j // 8, :, pl.ds(j % 8 * BLOCK, BLOCK)] = kept.astype(jnp.bfloat16)
    pl.semaphore_wait(barrier, len(greeted))

    def copy(src, dst, send, recv, peer):
        return pltpu.make_async_remote_copy(
            src_ref=src, dst_ref=dst, send_sem=send, recv_sem=recv, device_id=peer, device_id_type=MESH
        )

    def a_up(s, d):
        k = zl - d
        return copy(a_slab.at[s, k], a_slab.at[s, k], a_plus.at[s, d], a_recv.at[s, k], {"col": zl + 1})

    def a_down(s, d):
        k = zl + d
        return copy(a_slab.at[s, k], a_slab.at[s, k], a_minus.at[s, d], a_recv.at[s, k], {"col": zl - 1})

    def up_sends(d):
        return jnp.logical_and(zl >= d, zl < 3)

    def down_sends(d):
        return jnp.logical_and(zl + d <= 3, zl > 0)

    def a_own(s):
        pl.when(up_sends(0))(lambda: a_up(s, 0).start())
        pl.when(down_sends(0))(lambda: a_down(s, 0).start())

    def a_wait(s, d, sign):
        k = zl + sign * d
        copy(a_slab.at[s, k], a_slab.at[s, k], a_plus.at[s, 0], a_recv.at[s, k], {"col": zl}).wait_recv()

    def g_stage(s):
        for d in (1, 2):
            @pl.when(up_sends(d))
            def _():
                a_wait(s, d, -1)
                a_up(s, d).start()

            @pl.when(down_sends(d))
            def _():
                a_wait(s, d, 1)
                a_down(s, d).start()
        if s + 2 < STEPS:
            a_own(s + 2)

    def a_stage(s):
        for d in (1, 2, 3):
            for sign, sends in ((-1, up_sends), (1, down_sends)):
                here = jnp.logical_and(zl + sign * d >= 0, zl + sign * d <= 3)
                if d < 3:
                    here = jnp.logical_and(here, jnp.logical_not(sends(d)))
                pl.when(here)(lambda: a_wait(s, d, sign))

    def chunk(shift):
        return ((x + shift + 4) % 4) * 2 + core

    def b_copy(shift, h, q, sem, peer, recv):
        c = chunk(shift)
        return copy(b_slab.at[c, h, q], b_slab.at[c, h, q], sem, recv.at[c, h, q], peer)

    def b_to_plus(shift, h, q, n):
        return b_copy(shift, h, q, b_plus.at[q, n], x_peer(1), b_recv)

    def b_to_minus(shift, h, q, n):
        return b_copy(shift, h, q, b_minus.at[q, n], x_peer(-1), b_recv)

    def b_to_twin(shift, h, q):
        return b_copy(shift, h, q, b_twin.at[q, shift + 1, h], twin, b_twin_recv)

    def b_wait(shift, h, q):
        b_copy(shift, h, q, b_plus.at[q, 0], x_peer(1), b_recv).wait_recv()

    def b_own(q):
        for h in range(2):
            b_to_plus(0, h, q, h).start()
            b_to_minus(0, 1 - h, q, h).start()

    def e_stage(n, q):
        if n == 1:
            b_wait(-1, 0, q)
            b_to_plus(-1, 0, q, 2).start()
            b_wait(1, 1, q)
            b_to_minus(1, 1, q, 2).start()
            b_to_twin(-1, 0, q).start()
            b_to_twin(1, 1, q).start()
            if q == 0:
                b_own(1)
                for h in range(2):
                    b_to_twin(0, h, 1).start()
        elif n == 2:
            b_wait(-1, 1, q)
            b_to_twin(-1, 1, q).start()
            b_wait(1, 0, q)
            b_to_twin(1, 0, q).start()
        else:
            b_wait(2, 0, q)
            b_to_twin(2, 0, q).start()
            b_wait(2, 1, q)
            b_to_twin(2, 1, q).start()
            for other in range(4):
                for h in range(2):
                    c = other * 2 + 1 - core
                    copy(b_slab.at[c, h, q], b_slab.at[c, h, q], b_plus.at[q, 0], b_twin_recv.at[c, h, q],
                         twin).wait_recv()

    def y_data(s, q, shift):
        return copy(sent.at[s, q, (y + shift) % 4], got.at[s, q, shift - 1], y_send.at[s, q, shift - 1],
                    y_recv.at[s, q, shift - 1], y_peer(shift))

    def y_scale(s, q, shift):
        return copy(sent_scale.at[s, q], got_scale.at[s, q, shift - 1], y_send_s.at[s, q, shift - 1],
                    y_recv_s.at[s, q, shift - 1], y_peer(shift))

    def coded(values, axes):
        most = jnp.maximum(jnp.max(jnp.abs(values), axis=axes, keepdims=True), TINY)
        codes = jnp.round(values * (LEVELS / most)).astype(jnp.int16)
        return codes, most * (1.0 / LEVELS)

    def c_stage(s, q):
        @pl.loop(0, HALF // TILE)
        def _(n):
            cols = pl.ds(pl.multiple_of(n * TILE, TILE), TILE)
            total = jnp.zeros((BLOCK, TILE), jnp.float32)
            for k in range(4):
                total += jnp.dot(
                    a_slab[s, k].reshape(BLOCK, 512),
                    b_slab[2 * k:2 * k + 2, :, q, :, cols].reshape(512, TILE),
                    preferred_element_type=jnp.float32,
                )
            part[:, :, :, cols] = total.reshape(4, 2, SUB, TILE)
            codes, scale = coded(total, 0)
            sent[s, q, :, :, :, cols] = codes.reshape(4, 2, SUB, TILE)
            sent_scale[s, q, :, cols] = scale

        held[s, q] = part[y]
        for shift in (2, 1, 3):
            y_data(s, q, shift).start()
            y_scale(s, q, shift).start()

    def d_stage(s):
        for q in range(2):
            for shift in (2, 1, 3):
                y_data(s, q, shift).wait_recv()
                y_scale(s, q, shift).wait_recv()
            mine = held[s, q, zh]
            theirs = held[s, q, 1 - zh]
            for n in range(3):
                mine += got[s, q, n, zh].astype(jnp.float32) * got_scale[s, q, n]
                theirs += got[s, q, n, 1 - zh].astype(jnp.float32) * got_scale[s, q, n]
            held[s, q, zh] = mine
            codes, scale = coded(theirs, 0)
            z_sent[s, q] = codes
            z_sent_scale[s, q] = scale

    def z_data(s):
        return copy(z_sent.at[s], z_got.at[s], z_send.at[s], z_recv.at[s], z_peer)

    def z_scale(s):
        return copy(z_sent_scale.at[s], z_got_scale.at[s], z_send_s.at[s], z_recv_s.at[s], z_peer)

    def z_stage(s):
        z_data(s).start()
        z_scale(s).start()

    def f_stage(s):
        z_data(s).wait_recv()
        z_scale(s).wait_recv()
        for q in range(2):
            out_ref[s, :, q * HALF:(q + 1) * HALF] = (
                held[s, q, zh] + z_got[s, q].astype(jnp.float32) * z_got_scale[s, q]
            )

    a_own(0)
    b_own(0)
    a_own(1)
    for h in range(2):
        b_to_twin(0, h, 0).start()
    stages = {"A": a_stage, "C": c_stage, "D": d_stage, "E": e_stage, "F": f_stage, "G": g_stage, "Z": z_stage}
    for name in ORDER:
        halves = ("LR".index(name[2]),) if name[2:] else ()
        stages[name[0]](int(name[1]), *halves)

    for s in range(STEPS):
        for d in range(3):
            pl.when(up_sends(d))(lambda: a_up(s, d).wait_send())
            pl.when(down_sends(d))(lambda: a_down(s, d).wait_send())
        for q in range(2):
            for shift in (1, 2, 3):
                y_data(s, q, shift).wait_send()
                y_scale(s, q, shift).wait_send()
        z_data(s).wait_send()
        z_scale(s).wait_send()
    for q in range(2):
        for n in range(3):
            b_to_plus(0, 0, q, n).wait_send()
            b_to_minus(0, 0, q, n).wait_send()
        for shift in (-1, 0, 1, 2):
            for h in range(2):
                b_to_twin(shift, h, q).wait_send()


def per_device(a_tiles, a_occupancy, b_tiles, b_occupancy):
    vmem = pl.BlockSpec(memory_space=pltpu.VMEM)
    smem = pl.BlockSpec(memory_space=pltpu.SMEM)
    sems = pltpu.SemaphoreType.DMA
    out = pl.pallas_call(
        kernel,
        out_shape=jax.ShapeDtypeStruct((STEPS, SUB, 2048), jnp.float32),
        in_specs=[smem, smem, vmem, vmem],
        out_specs=vmem,
        scratch_shapes=[
            pltpu.VMEM((STEPS, 4, 8, SUB, 512), jnp.bfloat16),
            pltpu.VMEM((8, 2, 2, BLOCK, HALF), jnp.bfloat16),
            pltpu.VMEM((4, 2, SUB, HALF), jnp.float32),
            pltpu.VMEM((STEPS, 2, 4, 2, SUB, HALF), jnp.int16),
            pltpu.VMEM((STEPS, 2, 1, HALF), jnp.float32),
            pltpu.VMEM((STEPS, 2, 3, 2, SUB, HALF), jnp.int16),
            pltpu.VMEM((STEPS, 2, 3, 1, HALF), jnp.float32),
            pltpu.VMEM((STEPS, 2, 2, SUB, HALF), jnp.float32),
            pltpu.VMEM((STEPS, 2, SUB, HALF), jnp.int16),
            pltpu.VMEM((STEPS, 2, 1, HALF), jnp.float32),
            pltpu.VMEM((STEPS, 2, SUB, HALF), jnp.int16),
            pltpu.VMEM((STEPS, 2, 1, HALF), jnp.float32),
            sems((STEPS, 3)), sems((STEPS, 3)), sems((STEPS, 4)),
            sems((2, 3)), sems((2, 3)), sems((2, 4, 2)), sems((8, 2, 2)), sems((8, 2, 2)),
            sems((STEPS, 2, 3)), sems((STEPS, 2, 3)), sems((STEPS, 2, 3)), sems((STEPS, 2, 3)),
            sems((STEPS,)), sems((STEPS,)), sems((STEPS,)), sems((STEPS,)),
        ],
        compiler_params=pltpu.CompilerParams(
            collective_id=0, has_side_effects=True, vmem_limit_bytes=56 << 20
        ),
    )(a_occupancy.T, b_occupancy, a_tiles.reshape(8, STEPS, SUB, 512), b_tiles)
    return out.reshape(BLOCK, 2048)


def solution(mesh):
    in_specs = (
        P("row", ("layer", "col")),
        P("row", ("layer", "col")),
        P(("layer", "row"), "col"),
        P(("layer", "row"), "col"),
    )
    out_specs = P(("row", "layer"), "col")
    return jax.shard_map(
        per_device, mesh=mesh, in_specs=in_specs, out_specs=out_specs, check_vma=False
    )
```

time: 355 us -> 119 us (0.34)
  the two profiles are of different devices: /device:TPU:1 before, /device:TPU:32 now
where the time goes in v1:
time: 119 us
  Pallas kernels  117 us (98%)
  local copies, waits for them, and re-layouts  2.3 us (2%)
    pallas_call x1, Pallas kernels, per_device(): pl.pallas_call(kernel, out_shape=jax.ShapeDtypeStruct((STEPS, SUB, 2048),...  117 us

profile of v1, /device:TPU:32, one launch (start us, length us, event | category | flops | bytes accessed | tf_op | source)
XLA Modules:
  0.0 119.2 jit_solution(14875321112561164919)
XLA Ops:
  0.0 116.9 %shard_map.46 = f32[8,16,2048]{2,1,0:T(8,128)} custom-call(s32[4,8]{1,0:T(4,128)} %bitcast.5, s32[2,16]{1,0:T(2,128)} %b_occ.1, bf16[8,8,16,512]{3,2,1,0:T(8,128)(2,1)} %bitcast.4, bf16[256,2048]{1,0:T(8,128)(2,1)} %b_ref.1), custom_call_target="tpu_custom_call" | custom-call | tf_op jit(solution)/shard_map/pallas_call | solution.py:268
  116.9 2.3 %copy.6 = f32[128,2048]{1,0:T(8,128)} copy(f32[128,2048]{1,0:T(8,128)} %bitcast.3) | data formatting | bytes 2097152

commit v2 on v1

--- a/solution.py
+++ b/solution.py
@@ -16,12 +16,12 @@
 TILE = 256
 HALF = 1024
 ORDER = (
-    "E1L", "G0", "E2L", "G1", "E3L", "A0", "C0L", "A1", "C1L", "G2", "E1R", "G3",
-    "A2", "C2L", "E2R", "G4", "G5", "A3", "C3L", "E3R", "C0R", "C1R", "C2R", "C3R",
-    "G6", "G7", "A4", "C4L", "C4R", "A5", "C5L", "C5R", "D0", "D1", "A6", "C6L",
-    "C6R", "D2", "D3", "Z0", "Z1", "Z2", "Z3", "A7", "C7L", "C7R", "D4", "Z4",
-    "D5", "Z5", "D6", "Z6", "D7", "Z7", "F0", "F1", "F2", "F3", "F4", "F5",
-    "F6", "F7",
+    "G0", "E1L", "G1", "E2L", "E3L", "A1", "G2", "A2", "A0", "C2L", "E1R", "C1L",
+    "G3", "C0L", "E2R", "A3", "C3L", "E3R", "G4", "C0R", "C2R", "A4", "G5", "C3R",
+    "C1R", "A5", "D0", "Z0", "C4R", "G6", "C4L", "C5L", "D3", "C5R", "Z3", "G7",
+    "A6", "C6L", "D1", "D4", "D2", "Z1", "Z4", "C6R", "A7", "F3", "Z2", "C7L",
+    "D5", "F0", "C7R", "D6", "Z5", "Z6", "F4", "D7", "Z7", "F6", "F1", "F2",
+    "F5", "F7",
 )
 
 
@@ -71,11 +71,11 @@
 
     def a_up(s, d):
         k = zl - d
-        return copy(a_slab.at[s, k], a_slab.at[s, k], a_plus.at[s, d], a_recv.at[s, k], {"col": zl + 1})
+        return copy(a_slab.at[s, k], a_slab.at[s, k], a_plus.at[d], a_recv.at[s, k], {"col": zl + 1})
 
     def a_down(s, d):
         k = zl + d
-        return copy(a_slab.at[s, k], a_slab.at[s, k], a_minus.at[s, d], a_recv.at[s, k], {"col": zl - 1})
+        return copy(a_slab.at[s, k], a_slab.at[s, k], a_minus.at[d], a_recv.at[s, k], {"col": zl - 1})
 
     def up_sends(d):
         return jnp.logical_and(zl >= d, zl < 3)
@@ -89,7 +89,7 @@
 
     def a_wait(s, d, sign):
         k = zl + sign * d
-        copy(a_slab.at[s, k], a_slab.at[s, k], a_plus.at[s, 0], a_recv.at[s, k], {"col": zl}).wait_recv()
+        copy(a_slab.at[s, k], a_slab.at[s, k], a_plus.at[0], a_recv.at[s, k], {"col": zl}).wait_recv()
 
     def g_stage(s):
         for d in (1, 2):
@@ -118,31 +118,31 @@
 
     def b_copy(shift, h, q, sem, peer, recv):
         c = chunk(shift)
-        return copy(b_slab.at[c, h, q], b_slab.at[c, h, q], sem, recv.at[c, h, q], peer)
-
-    def b_to_plus(shift, h, q, n):
-        return b_copy(shift, h, q, b_plus.at[q, n], x_peer(1), b_recv)
-
-    def b_to_minus(shift, h, q, n):
-        return b_copy(shift, h, q, b_minus.at[q, n], x_peer(-1), b_recv)
+        return copy(b_slab.at[c, h, q], b_slab.at[c, h, q], sem, recv, peer)
+
+    def b_to_plus(shift, h, q):
+        return b_copy(shift, h, q, b_plus, x_peer(1), b_recv.at[(x + shift + 4) % 4, h, q])
+
+    def b_to_minus(shift, h, q):
+        return b_copy(shift, h, q, b_minus, x_peer(-1), b_recv.at[(x + shift + 4) % 4, h, q])
 
     def b_to_twin(shift, h, q):
-        return b_copy(shift, h, q, b_twin.at[q, shift + 1, h], twin, b_twin_recv)
+        return b_copy(shift, h, q, b_twin, twin, b_twin_recv.at[q])
 
     def b_wait(shift, h, q):
-        b_copy(shift, h, q, b_plus.at[q, 0], x_peer(1), b_recv).wait_recv()
+        b_copy(shift, h, q, b_plus, x_peer(1), b_recv.at[(x + shift + 4) % 4, h, q]).wait_recv()
 
     def b_own(q):
         for h in range(2):
-            b_to_plus(0, h, q, h).start()
-            b_to_minus(0, 1 - h, q, h).start()
+            b_to_plus(0, h, q).start()
+            b_to_minus(0, 1 - h, q).start()
 
     def e_stage(n, q):
         if n == 1:
             b_wait(-1, 0, q)
-            b_to_plus(-1, 0, q, 2).start()
+            b_to_plus(-1, 0, q).start()
             b_wait(1, 1, q)
-            b_to_minus(1, 1, q, 2).start()
+            b_to_minus(1, 1, q).start()
             b_to_twin(-1, 0, q).start()
             b_to_twin(1, 1, q).start()
             if q == 0:
@@ -159,19 +159,16 @@
             b_to_twin(2, 0, q).start()
             b_wait(2, 1, q)
             b_to_twin(2, 1, q).start()
-            for other in range(4):
-                for h in range(2):
-                    c = other * 2 + 1 - core
-                    copy(b_slab.at[c, h, q], b_slab.at[c, h, q], b_plus.at[q, 0], b_twin_recv.at[c, h, q],
-                         twin).wait_recv()
+            eight = b_slab.at[0:4, :, 0]
+            copy(eight, eight, b_plus, b_twin_recv.at[q], twin).wait_recv()
 
     def y_data(s, q, shift):
-        return copy(sent.at[s, q, (y + shift) % 4], got.at[s, q, shift - 1], y_send.at[s, q, shift - 1],
-                    y_recv.at[s, q, shift - 1], y_peer(shift))
+        return copy(sent.at[s, q, (y + shift) % 4], got.at[s, q, shift - 1], y_send,
+                    y_recv.at[s], y_peer(shift))
 
     def y_scale(s, q, shift):
-        return copy(sent_scale.at[s, q], got_scale.at[s, q, shift - 1], y_send_s.at[s, q, shift - 1],
-                    y_recv_s.at[s, q, shift - 1], y_peer(shift))
+        return copy(sent_scale.at[s, q], got_scale.at[s, q, shift - 1], y_send_s,
+                    y_recv_s.at[s], y_peer(shift))
 
     def coded(values, axes):
         most = jnp.maximum(jnp.max(jnp.abs(values), axis=axes, keepdims=True), TINY)
@@ -200,10 +197,9 @@
             y_scale(s, q, shift).start()
 
     def d_stage(s):
+        copy(got.at[s], got.at[s], y_send, y_recv.at[s], y_peer(1)).wait_recv()
+        copy(got_scale.at[s], got_scale.at[s], y_send_s, y_recv_s.at[s], y_peer(1)).wait_recv()
         for q in range(2):
-            for shift in (2, 1, 3):
-                y_data(s, q, shift).wait_recv()
-                y_scale(s, q, shift).wait_recv()
             mine = held[s, q, zh]
             theirs = held[s, q, 1 - zh]
             for n in range(3):
@@ -215,10 +211,10 @@
             z_sent_scale[s, q] = scale
 
     def z_data(s):
-        return copy(z_sent.at[s], z_got.at[s], z_send.at[s], z_recv.at[s], z_peer)
+        return copy(z_sent.at[s], z_got.at[s], z_send, z_recv.at[s], z_peer)
 
     def z_scale(s):
-        return copy(z_sent_scale.at[s], z_got_scale.at[s], z_send_s.at[s], z_recv_s.at[s], z_peer)
+        return copy(z_sent_scale.at[s], z_got_scale.at[s], z_send_s, z_recv_s.at[s], z_peer)
 
     def z_stage(s):
         z_data(s).start()
@@ -242,23 +238,19 @@
         halves = ("LR".index(name[2]),) if name[2:] else ()
         stages[name[0]](int(name[1]), *halves)
 
-    for s in range(STEPS):
-        for d in range(3):
-            pl.when(up_sends(d))(lambda: a_up(s, d).wait_send())
-            pl.when(down_sends(d))(lambda: a_down(s, d).wait_send())
-        for q in range(2):
-            for shift in (1, 2, 3):
-                y_data(s, q, shift).wait_send()
-                y_scale(s, q, shift).wait_send()
-        z_data(s).wait_send()
-        z_scale(s).wait_send()
-    for q in range(2):
-        for n in range(3):
-            b_to_plus(0, 0, q, n).wait_send()
-            b_to_minus(0, 0, q, n).wait_send()
-        for shift in (-1, 0, 1, 2):
-            for h in range(2):
-                b_to_twin(shift, h, q).wait_send()
+    def all_left(ref, sem):
+        copy(ref, ref, sem, z_recv.at[0], z_peer).wait_send()
+
+    for d in range(3):
+        pl.when(up_sends(d))(lambda: all_left(a_slab.at[:, 0], a_plus.at[d]))
+        pl.when(down_sends(d))(lambda: all_left(a_slab.at[:, 0], a_minus.at[d]))
+    all_left(b_slab.at[0:3, 0], b_plus)
+    all_left(b_slab.at[0:3, 0], b_minus)
+    all_left(b_slab.at[0:4], b_twin)
+    all_left(got, y_send)
+    all_left(got_scale, y_send_s)
+    all_left(z_got, z_send)
+    all_left(z_got_scale, z_send_s)
 
 
 def per_device(a_tiles, a_occupancy, b_tiles, b_occupancy):
@@ -283,10 +275,10 @@
             pltpu.VMEM((STEPS, 2, 1, HALF), jnp.float32),
             pltpu.VMEM((STEPS, 2, SUB, HALF), jnp.int16),
             pltpu.VMEM((STEPS, 2, 1, HALF), jnp.float32),
-            sems((STEPS, 3)), sems((STEPS, 3)), sems((STEPS, 4)),
-            sems((2, 3)), sems((2, 3)), sems((2, 4, 2)), sems((8, 2, 2)), sems((8, 2, 2)),
-            sems((STEPS, 2, 3)), sems((STEPS, 2, 3)), sems((STEPS, 2, 3)), sems((STEPS, 2, 3)),
-            sems((STEPS,)), sems((STEPS,)), sems((STEPS,)), sems((STEPS,)),
+            sems((3,)), sems((3,)), sems((STEPS, 4)),
+            sems, sems, sems, sems((4, 2, 2)), sems((2,)),
+            sems, sems((STEPS,)), sems, sems((STEPS,)),
+            sems, sems((STEPS,)), sems, sems((STEPS,)),
         ],
         compiler_params=pltpu.CompilerParams(
             collective_id=0, has_side_effects=True, vmem_limit_bytes=56 << 20

time: 119 us -> 112 us (0.941)
  the two profiles are of different devices: /device:TPU:32 before, /device:TPU:1 now
where the time goes in v2:
time: 112 us
  Pallas kernels  110 us (98%)
  local copies, waits for them, and re-layouts  2.3 us (2%)
    pallas_call x1, Pallas kernels, per_device(): pl.pallas_call(kernel, out_shape=jax.ShapeDtypeStruct((STEPS, SUB, 2048),...  110 us
    unnamed x1, local copies, waits for them, and re-layouts  2.3 us

profile of v2, /device:TPU:1, one launch (start us, length us, event | category | flops | bytes accessed | tf_op | source)
XLA Modules:
  0.0 112.1 jit_solution(13035542508011691599)
XLA Ops:
  0.0 109.8 %shard_map.46 = f32[8,16,2048]{2,1,0:T(8,128)} custom-call(s32[4,8]{1,0:T(4,128)} %bitcast.5, s32[2,16]{1,0:T(2,128)} %b_occ.1, bf16[8,8,16,512]{3,2,1,0:T(8,128)(2,1)} %bitcast.4, bf16[256,2048]{1,0:T(8,128)(2,1)} %b_ref.1), custom_call_target="tpu_custom_call" | custom-call | tf_op jit(solution)/shard_map/pallas_call | solution.py:260
  109.8 2.3 %copy.6 = f32[128,2048]{1,0:T(8,128)} copy(f32[128,2048]{1,0:T(8,128)} %bitcast.3) | data formatting | bytes 2097152

commit v3 on v2

--- a/solution.py
+++ b/solution.py
@@ -199,6 +199,7 @@
     def d_stage(s):
         copy(got.at[s], got.at[s], y_send, y_recv.at[s], y_peer(1)).wait_recv()
         copy(got_scale.at[s], got_scale.at[s], y_send_s, y_recv_s.at[s], y_peer(1)).wait_recv()
+        rest = []
         for q in range(2):
             mine = held[s, q, zh]
             theirs = held[s, q, 1 - zh]
@@ -206,9 +207,17 @@
                 mine += got[s, q, n, zh].astype(jnp.float32) * got_scale[s, q, n]
                 theirs += got[s, q, n, 1 - zh].astype(jnp.float32) * got_scale[s, q, n]
             held[s, q, zh] = mine
-            codes, scale = coded(theirs, 0)
-            z_sent[s, q] = codes
-            z_sent_scale[s, q] = scale
+            rest.append(theirs)
+        most = jnp.max(jnp.maximum(jnp.abs(rest[0]), jnp.abs(rest[1])), axis=0, keepdims=True)
+        lanes = [most[:, n * BLOCK:(n + 1) * BLOCK] for n in range(HALF // BLOCK)]
+        peak = jnp.maximum(functools.reduce(jnp.maximum, lanes), TINY)
+        wide = spread(LEVELS / peak)
+        for q in range(2):
+            z_sent[s, q] = jnp.round(rest[q] * wide).astype(jnp.int16)
+        z_sent_scale[s] = peak * (1.0 / LEVELS)
+
+    def spread(lanes):
+        return jnp.concatenate([lanes] * (HALF // BLOCK), axis=1)
 
     def z_data(s):
         return copy(z_sent.at[s], z_got.at[s], z_send, z_recv.at[s], z_peer)
@@ -225,7 +234,7 @@
         z_scale(s).wait_recv()
         for q in range(2):
             out_ref[s, :, q * HALF:(q + 1) * HALF] = (
-                held[s, q, zh] + z_got[s, q].astype(jnp.float32) * z_got_scale[s, q]
+                held[s, q, zh] + z_got[s, q].astype(jnp.float32) * spread(z_got_scale[s])
             )
 
     a_own(0)
@@ -272,9 +281,9 @@
             pltpu.VMEM((STEPS, 2, 3, 1, HALF), jnp.float32),
             pltpu.VMEM((STEPS, 2, 2, SUB, HALF), jnp.float32),
             pltpu.VMEM((STEPS, 2, SUB, HALF), jnp.int16),
-            pltpu.VMEM((STEPS, 2, 1, HALF), jnp.float32),
+            pltpu.VMEM((STEPS, 1, BLOCK), jnp.float32),
             pltpu.VMEM((STEPS, 2, SUB, HALF), jnp.int16),
-            pltpu.VMEM((STEPS, 2, 1, HALF), jnp.float32),
+            pltpu.VMEM((STEPS, 1, BLOCK), jnp.float32),
             sems((3,)), sems((3,)), sems((STEPS, 4)),
             sems, sems, sems, sems((4, 2, 2)), sems((2,)),
             sems, sems((STEPS,)), sems, sems((STEPS,)),

time: 112 us -> 110 us (0.982)
  Pallas kernels: 110 us -> 107 us
    pallas_call x1, Pallas kernels: 110 us -> 107 us  [per_device(): pl.pallas_call(kernel, out_shape=jax.ShapeDtypeStruct((STEPS, SUB, 2048),...]
where the time goes in v3:
time: 110 us
  Pallas kernels  107 us (97%)
  local copies, waits for them, and re-layouts  2.3 us (2%)
    pallas_call x1, Pallas kernels, per_device(): pl.pallas_call(kernel, out_shape=jax.ShapeDtypeStruct((STEPS, SUB, 2048),...  107 us
    unnamed x1, local copies, waits for them, and re-layouts  2.3 us

profile of v3, /device:TPU:1, one launch (start us, length us, event | category | flops | bytes accessed | tf_op | source)
XLA Modules:
  0.0 109.6 jit_solution(1492257796648179835)
XLA Ops:
  0.0 107.3 %shard_map.46 = f32[8,16,2048]{2,1,0:T(8,128)} custom-call(s32[4,8]{1,0:T(4,128)} %bitcast.5, s32[2,16]{1,0:T(2,128)} %b_occ.1, bf16[8,8,16,512]{3,2,1,0:T(8,128)(2,1)} %bitcast.4, bf16[256,2048]{1,0:T(8,128)(2,1)} %b_ref.1), custom_call_target="tpu_custom_call" | custom-call | tf_op jit(solution)/shard_map/pallas_call | solution.py:269
  107.3 2.3 %copy.6 = f32[128,2048]{1,0:T(8,128)} copy(f32[128,2048]{1,0:T(8,128)} %bitcast.3) | data formatting | bytes 2097152

commit v4 on v3

--- a/solution.py
+++ b/solution.py
@@ -19,9 +19,9 @@
     "G0", "E1L", "G1", "E2L", "E3L", "A1", "G2", "A2", "A0", "C2L", "E1R", "C1L",
     "G3", "C0L", "E2R", "A3", "C3L", "E3R", "G4", "C0R", "C2R", "A4", "G5", "C3R",
     "C1R", "A5", "D0", "Z0", "C4R", "G6", "C4L", "C5L", "D3", "C5R", "Z3", "G7",
-    "A6", "C6L", "D1", "D4", "D2", "Z1", "Z4", "C6R", "A7", "F3", "Z2", "C7L",
-    "D5", "F0", "C7R", "D6", "Z5", "Z6", "F4", "D7", "Z7", "F6", "F1", "F2",
-    "F5", "F7",
+    "A6", "C6L", "D1", "D4", "D2", "Z1", "Z4", "C6R", "A7", "Z2", "C7L", "D5",
+    "Z5", "C7R", "D6", "Z6", "D7", "Z7", "F0", "F3", "F1", "F2", "F4", "F5",
+    "F6", "F7",
 )
 
 
@@ -102,8 +102,8 @@
             def _():
                 a_wait(s, d, 1)
                 a_down(s, d).start()
-        if s + 2 < STEPS:
-            a_own(s + 2)
+        if s + 3 < STEPS:
+            a_own(s + 3)
 
     def a_stage(s):
         for d in (1, 2, 3):
@@ -240,6 +240,7 @@
     a_own(0)
     b_own(0)
     a_own(1)
+    a_own(2)
     for h in range(2):
         b_to_twin(0, h, 0).start()
     stages = {"A": a_stage, "C": c_stage, "D": d_stage, "E": e_stage, "F": f_stage, "G": g_stage, "Z": z_stage}

time: 110 us -> 109 us (level)
    pallas_call x1, Pallas kernels: 107 us -> 106 us  [per_device(): pl.pallas_call(kernel, out_shape=jax.ShapeDtypeStruct((STEPS, SUB, 2048),...]
where the time goes in v4:
time: 109 us; the launch traced here: 108 us
  Pallas kernels  106 us (97%)
  local copies, waits for them, and re-layouts  2.3 us (2%)
    pallas_call x1, Pallas kernels, per_device(): pl.pallas_call(kernel, out_shape=jax.ShapeDtypeStruct((STEPS, SUB, 2048),...  106 us
    unnamed x1, local copies, waits for them, and re-layouts  2.3 us

profile of v4, /device:TPU:1, one launch (start us, length us, event | category | flops | bytes accessed | tf_op | source)
XLA Modules:
  0.0 108.0 jit_solution(15536142391225067696)
XLA Ops:
  0.0 105.7 %shard_map.46 = f32[8,16,2048]{2,1,0:T(8,128)} custom-call(s32[4,8]{1,0:T(4,128)} %bitcast.5, s32[2,16]{1,0:T(2,128)} %b_occ.1, bf16[8,8,16,512]{3,2,1,0:T(8,128)(2,1)} %bitcast.4, bf16[256,2048]{1,0:T(8,128)(2,1)} %b_ref.1), custom_call_target="tpu_custom_call" | custom-call | tf_op jit(solution)/shard_map/pallas_call | solution.py:270
  105.7 2.3 %copy.6 = f32[128,2048]{1,0:T(8,128)} copy(f32[128,2048]{1,0:T(8,128)} %bitcast.3) | data formatting | bytes 2097152
